TPU v7x, 32 devices: a whole 2x2x4 slice. The times are simulated.
32 devices in a mesh: groups: 2 (over y), frame: 8 (over z, x), row: 2 (over core).
Axes of the slice: x: 2, y: 2, z: 4, core: 2. Of those that a mesh axis runs over, the one named last changes fastest.
Arguments:
- latent: bfloat16 [16, 16, 64, 640], P(('groups', 'frame'), 'row'), parts along dimension 0, may hold values from -18 to 18
- norm_gain: float32 [640], replicated, may hold values from 0.1 to 1.9
- time_kernel: bfloat16 [3, 640, 640], replicated, may hold values from -0.125 to 0.125
- space_norm: float32 [640], replicated, may hold values from 0.1 to 1.9
- space_qkv: bfloat16 [640, 1920], replicated, may hold values from -12 to 12
- space_out: bfloat16 [640, 640], replicated, may hold values from -0.25 to 0.25
- time_norm: float32 [640], replicated, may hold values from 0.1 to 1.9
- time_qkv: bfloat16 [640, 1920], replicated, may hold values from -12 to 12
- time_out: bfloat16 [640, 640], replicated, may hold values from -0.25 to 0.25
Outputs:
- output: float32 [16, 16, 64, 640], P(('groups', 'frame'), 'row'), parts along dimension 0
There are 2 independent parts, one for each index of `groups`. A program takes and returns all parts, laid end to end along the dimension named above; an argument that names none is the same for every part. Nothing has to cross between parts.
All inputs are finite; a program needn't handle non-finite values.
Results may differ from a plain program's by a relative error of at most 0.0018.
Values may be sent and summed in bfloat16 or wider, within the bound.
A program may use at most 128 MiB of HBM per device.

v0:
```python
import jax
import jax.numpy as jnp
from jax import lax
from jax.sharding import PartitionSpec as P

HEADS = 10
GROUPS = 32
epsilon = 1e-05


def padded_2(block, sides, width):
    for axis, dim in sides:
        count = lax.axis_size(axis)
        forward = [(i, i + 1) for i in range(count - 1)]
        backward = [(target, source) for source, target in forward]
        low = lax.ppermute(
            lax.slice_in_dim(block, block.shape[dim] - width, None, axis=dim), axis, forward
        )
        high = lax.ppermute(lax.slice_in_dim(block, 0, width, axis=dim), axis, backward)
        block = jnp.concatenate([low, block, high], axis=dim)
    return block


def normalize_silu(grouped, first, second, number, gain, shape):
    center = first / number
    spread = second / number - center * center
    scaling = lax.rsqrt(spread + epsilon)
    normed = ((grouped - center[:, None]) * scaling[:, None]).reshape(shape) * gain
    return jax.nn.silu(normed).astype(jnp.bfloat16)


def layer_norm(inputs, gain):
    center = jnp.mean(inputs, axis=-1, keepdims=True)
    shifted = inputs - center
    spread = jnp.mean(shifted * shifted, axis=-1, keepdims=True)
    return (shifted * lax.rsqrt(spread + epsilon) * gain).astype(jnp.bfloat16)


def project_three(inputs, weight):
    channels = weight.shape[0]
    lead = inputs.shape[:-1]
    packed = jnp.dot(
        inputs.reshape(-1, channels), weight, preferred_element_type=jnp.float32
    ).astype(jnp.bfloat16)
    packed = packed.reshape(lead + (3 * channels,))
    return (
        packed[..., :channels],
        packed[..., channels : 2 * channels],
        packed[..., 2 * channels :],
    )


def time_attend(queries, key_rows, values):
    frames, pixels, channels = queries.shape
    head_size = channels // HEADS
    query_heads = queries.reshape(frames, pixels, HEADS, head_size)
    key_heads = key_rows.reshape(frames, pixels, HEADS, head_size)
    value_heads = values.reshape(frames, pixels, HEADS, head_size)
    scores = jnp.einsum(
        "qphd,kphd->phqk", query_heads, key_heads, preferred_element_type=jnp.float32
    ) * head_size ** (-0.5)
    raised = jnp.exp(scores - jnp.max(scores, axis=-1, keepdims=True))
    weight_sum = jnp.sum(raised, axis=-1)
    weights = raised.astype(jnp.bfloat16)
    result = jnp.einsum("phqk,kphd->qphd", weights, value_heads, preferred_element_type=jnp.float32)
    result = result / jnp.transpose(weight_sum, (2, 0, 1))[:, :, :, None]
    return result.astype(jnp.bfloat16).reshape(frames, pixels, channels)


def add_projected(base, attended, weight):
    channels = weight.shape[0]
    summed = base.reshape(-1, channels) + jnp.dot(
        attended.reshape(-1, channels), weight, preferred_element_type=jnp.float32
    )
    return summed.reshape(base.shape)


def body(
    latent, norm_gain, time_kernel, space_norm, space_qkv, space_out, time_norm, time_qkv, time_out
):
    frames, row_count, col_count, channels = latent.shape
    pixels = row_count * col_count
    per_group = channels // GROUPS
    head_size = channels // HEADS
    grouped = latent.astype(jnp.float32).reshape(frames, row_count, col_count, GROUPS, per_group)
    first = jnp.sum(grouped, axis=(0, 1, 2, 4))
    second = jnp.sum(grouped * grouped, axis=(0, 1, 2, 4))
    first, second = lax.psum((first, second), ("frame", "row"))
    number = frames * lax.axis_size("frame") * pixels * lax.axis_size("row") * per_group
    hidden = normalize_silu(grouped, first, second, number, norm_gain, latent.shape)
    padded = padded_2(hidden, (("frame", 0),), 1)
    mixed = jnp.zeros((frames * pixels, channels), jnp.float32)
    for tap in range(3):
        window = padded[tap : tap + frames].reshape(-1, channels)
        mixed = mixed + jnp.dot(window, time_kernel[tap], preferred_element_type=jnp.float32)
    stepped = latent.astype(jnp.float32).reshape(-1, channels) + mixed
    stepped = stepped.reshape(frames, pixels, channels)
    tokens = layer_norm(stepped, space_norm)
    queries, key_rows, values = project_three(tokens, space_qkv)
    query_heads = queries.reshape(frames, pixels, HEADS, head_size)
    top_score = jnp.full((frames, HEADS, pixels), -jnp.inf, jnp.float32)
    weight_sum = jnp.zeros((frames, HEADS, pixels), jnp.float32)
    partial_sum = jnp.zeros((frames, HEADS, pixels, head_size), jnp.float32)
    key_piece = lax.all_gather(key_rows, "row", axis=1, tiled=True)
    value_piece = lax.all_gather(values, "row", axis=1, tiled=True)
    key_count = key_piece.shape[1]
    key_heads = key_piece.reshape(frames, key_count, HEADS, head_size)
    value_heads = value_piece.reshape(frames, key_count, HEADS, head_size)
    scores = jnp.einsum(
        "fqhd,fkhd->fhqk", query_heads, key_heads, preferred_element_type=jnp.float32
    ) * head_size ** (-0.5)
    new_top = jnp.max(scores, axis=-1)
    rescale = jnp.exp(top_score - new_top)
    raised = jnp.exp(scores - new_top[..., None])
    weight_sum = weight_sum * rescale + jnp.sum(raised, axis=-1)
    weights = raised.astype(jnp.bfloat16)
    partial_sum = partial_sum * rescale[..., None] + jnp.einsum(
        "fhqk,fkhd->fhqd", weights, value_heads, preferred_element_type=jnp.float32
    )
    top_score, weight_sum, partial_sum = (new_top, weight_sum, partial_sum)
    attended = (partial_sum / weight_sum[..., None]).astype(jnp.bfloat16)
    attended = jnp.transpose(attended, (0, 2, 1, 3)).reshape(frames, pixels, channels)
    spaced = add_projected(stepped, attended, space_out)
    moved = lax.all_to_all(spaced, "frame", split_axis=1, concat_axis=0, tiled=True)
    normed = layer_norm(moved, time_norm)
    queries, key_rows, values = project_three(normed, time_qkv)
    result = time_attend(queries, key_rows, values)
    finished = add_projected(moved, result, time_out)
    output = lax.all_to_all(finished, "frame", split_axis=0, concat_axis=1, tiled=True)
    return output.reshape(frames, row_count, col_count, channels)


def solution(mesh):
    return jax.shard_map(
        body,
        mesh=mesh,
        in_specs=(
            P(("groups", "frame"), "row", None, None),
            P(),
            P(),
            P(),
            P(),
            P(),
            P(),
            P(),
            P(),
        ),
        out_specs=P(("groups", "frame"), "row", None, None),
        check_vma=False,
    )
```

profile of v0, /device:TPU:0, one launch (start us, length us, event | category | flops | bytes accessed | tf_op | source)
XLA Modules:
  0.0 232.8 jit_solution(14657514073746604664)
XLA Ops:
  6.5 1.4 convert_reduce_fusion
  8.4 34.9 %all-reduce = (f32[32]{0:T(128)S(1)}, f32[32]{0:T(128)S(1)}) all-reduce(f32[32]{0:T(128)S(1)} %reduce_sum.91, f32[32]{0:T(128)S(1)} %reduce_sum.88), channel_id=1, replica_groups=mesh['groups'=2,'frame'=8,'row'=2] {'frame','row'}, use_global_device_ids=true, to_apply=%region_5.6 | all-reduce | flops 64 | bytes 512 | tf_op jit(solution)/shard_map/psum | solution.py:88
  43.7 1.5 multiply_convert_fusion.1
  45.2 1.3 collective-permute-start.1
  46.5 4.6 %collective-permute-start = (bf16[1,8,64,640]{3,2,1,0:T(8,128)(2,1)S(1)}, bf16[1,8,64,640]{3,2,1,0:T(8,128)(2,1)S(1)}, u32[]{:S(2)}, u32[]{:S(2)}) collective-permute-start(bf16[1,8,64,640]{3,2,1,0:T(8,128)(2,1)S(1)} %multiply_convert_fusion.1), channel_id=1, source_target_pairs={{0,2},{2,4},{4,6},{6,8},{8,10},{10,12},{12,14},{1,3},{3,5},{5,7},{... | collective-permute-start | bytes 1966088 | tf_op jit(solution)/shard_map/ppermute | solution.py:16
  51.1 2.0 fusion.24
  53.2 6.7 %collective-permute-done.1 = bf16[1,8,64,640]{3,2,1,0:T(8,128)(2,1)S(1)} collective-permute-done((bf16[1,8,64,640]{3,2,1,0:T(8,128)(2,1)S(1)}, bf16[1,8,64,640]{3,2,1,0:T(8,128)(2,1)S(1)}, u32[]{:S(2)}, u32[]{:S(2)}) %collective-permute-start.1) | collective-permute-done | bytes 655392 | tf_op jit(solution)/shard_map/ppermute | solution.py:19
  60.6 8.8 %collective-permute-done = bf16[1,8,64,640]{3,2,1,0:T(8,128)(2,1)S(1)} collective-permute-done((bf16[1,8,64,640]{3,2,1,0:T(8,128)(2,1)S(1)}, bf16[1,8,64,640]{3,2,1,0:T(8,128)(2,1)S(1)}, u32[]{:S(2)}, u32[]{:S(2)}) %collective-permute-start) | collective-permute-done | bytes 655392 | tf_op jit(solution)/shard_map/ppermute | solution.py:16
  71.0 1.9 fusion.4
  74.9 10.5 %all-gather.3.cloned.1.call-done = bf16[1,1024,640]{2,1,0:T(8,128)(2,1)} async-done(((bf16[1,512,640]{2,1,0:T(8,128)(2,1)}), bf16[1,1024,640]{2,1,0:T(8,128)(2,1)}) %all-gather.3.cloned.1.call-update) | async-done | bytes 1310736 | tf_op jit(solution)/shard_map/all_gather | solution.py:104
  85.4 1.6 copy.26
  87.0 3.0 %multiply_reduce_fusion = (f32[10,512]{1,0:T(8,128)S(1)}, f32[10,512,1024]{2,1,0:T(8,128)S(1)}) fusion(bf16[512,10,64]{0,2,1:T(8,128)(2,1)S(1)} %bitcast.75, bf16[1024,10,64]{0,2,1:T(8,128)(2,1)S(1)} %bitcast.69), kind=kOutput, calls=%fused_computation.1 | convolution fusion | flops 681569280 | bytes 22958080 | tf_op jit(solution)/shard_map/fqhd,fkhd->fhqk/dot_general | solution.py:109
  90.0 4.6 %fusion = f32[10,512]{1,0:T(8,128)S(1)} fusion(f32[10,512,1024]{2,1,0:T(8,128)S(1)} %get-tuple-element.22, f32[10,512]{1,0:T(8,128)S(1)} %get-tuple-element.21), kind=kLoop, calls=%fused_computation.2 | loop fusion | flops 15723520 | bytes 21012480 | tf_op jit(solution)/shard_map/reduce_sum | solution.py:115
  94.6 3.0 %copy-done.2 = f32[10,512,1024]{2,1,0:T(8,128)} copy-done((f32[10,512,1024]{2,1,0:T(8,128)}, f32[10,512,1024]{2,1,0:T(8,128)S(1)}, u32[]{:S(2)}) %copy-start.2) | copy-done | bytes 20971544
  97.6 2.5 %copy.27 = bf16[1,1024,640]{1,2,0:T(8,128)(2,1)} copy(bf16[1,1024,640]{2,1,0:T(8,128)(2,1)} %all-gather.5.cloned.1.call-done) | data formatting | bytes 2621440 | tf_op jit(solution)/shard_map/all_gather | solution.py:105
  100.2 9.5 %divide_convert_fusion = bf16[10,512,64]{1,2,0:T(8,128)(2,1)S(1)} fusion(bf16[1024,10,64]{0,2,1:T(8,128)(2,1)} %bitcast.78, f32[10,512,1024]{2,1,0:T(8,128)} %copy-done.2, f32[10,512]{1,0:T(8,128)S(1)} %get-tuple-element.21, f32[10,512]{1,0:T(8,128)S(1)} %get-tuple-element.16, f32[10,512]{1,0:T(8,128)S(1)} %get-tuple-element.15), kind=kOutput, calls=%fused_computation.28 | convolution fusion | flops 687800320 | bytes 22999040 | tf_op jit(solution)/shard_map/fhqk,fkhd->fhqd/dot_general | solution.py:117
  110.5 1.3 copy.28
  111.9 37.4 %all_to_all.8 = f32[1,512,640]{2,0,1:T(1,128)S(1)} all-to-all(f32[1,512,640]{2,0,1:T(1,128)S(1)} %copy.28), channel_id=1, replica_groups=mesh['groups'=2,'frame'=8,'row'=2] {'frame'}, dimensions={1} | all-to-all | bytes 2621440 | tf_op jit(solution)/shard_map/all_to_all | solution.py:124
  149.3 1.6 reduce_sum.95
  150.9 7.6 %multiply_reduce_fusion.2 = f32[512]{0:T(512)S(1)} fusion(f32[1,512,640]{2,0,1:T(1,128)S(1)} %all_to_all.8, f32[512]{0:T(512)S(1)} %broadcast_multiply_fusion), kind=kLoop, calls=%fused_computation.27 | loop fusion | flops 982528 | bytes 1314816 | tf_op jit(solution)/shard_map/reduce_sum | solution.py:35
  158.5 3.6 %convolution_convert_fusion = bf16[512,1920]{1,0:T(8,128)(2,1)S(1)} fusion(bf16[640,1920]{1,0:T(8,128)(2,1)} %param.16, f32[1,512,640]{2,0,1:T(1,128)S(1)} %all_to_all.8, f32[640]{0:T(1024)S(1)} %copy-done.11, f32[512]{0:T(512)S(1)} %add_rsqrt_fusion, f32[512]{0:T(512)S(1)} %broadcast_multiply_fusion), kind=kOutput, calls=%fused_computation.5 | convolution fusion | flops 1260584960 | bytes 5741056 | tf_op jit(solution)/shard_map/dot_general | solution.py:42
  163.2 2.3 copy.40
  165.5 2.6 %copy.32 = bf16[8,64,10,64]{3,0,2,1:T(8,128)(2,1)} copy(bf16[8,64,10,64]{1,3,2,0:T(8,128)(2,1)} %bitcast.71) | data formatting | bytes 1310720 | tf_op jit(solution)/shard_map/reshape | solution.py:56
  168.2 1.4 copy.41
  169.6 2.6 %copy.33 = bf16[8,64,10,64]{3,0,2,1:T(8,128)(2,1)} copy(bf16[8,64,10,64]{1,3,2,0:T(8,128)(2,1)} %bitcast.72) | data formatting | bytes 1310720 | tf_op jit(solution)/shard_map/reshape | solution.py:57
  172.2 1.4 copy.39
  173.6 2.7 %copy.34 = bf16[8,64,10,64]{3,0,2,1:T(8,128)(2,1)} copy(bf16[8,64,10,64]{1,3,2,0:T(8,128)(2,1)} %bitcast.73) | data formatting | bytes 1310720 | tf_op jit(solution)/shard_map/reshape | solution.py:58
  176.3 2.9 %multiply_reduce_fusion.1 = (f32[64,10,8]{2,1,0:T(8,128)S(1)}, f32[64,10,8,8]{2,3,1,0:T(8,128)S(1)}) fusion(bf16[8,64,10,64]{3,0,2,1:T(8,128)(2,1)} %copy.32, bf16[8,64,10,64]{3,0,2,1:T(8,128)(2,1)} %copy.33), kind=kOutput, calls=%fused_computation.11 | convolution fusion | flops 5319680 | bytes 1495040 | tf_op jit(solution)/shard_map/qphd,kphd->phqk/dot_general | solution.py:59
  180.4 2.5 %fusion.5 = bf16[8,64,10,64]{3,0,2,1:T(8,128)(2,1)} fusion(bf16[8,64,10,64]{3,0,2,1:T(8,128)(2,1)S(1)} %copy-done.7, f32[64,10,8,8]{2,3,1,0:T(8,128)S(1)} %get-tuple-element.24, f32[8,64,10]{0,2,1:T(8,128)S(1)} %bitcast.82, f32[64,10,8]{2,1,0:T(8,128)S(1)} %get-tuple-element.23), kind=kOutput, calls=%fused_computation.9 | convolution fusion | flops 6021120 | bytes 1515520 | tf_op jit(solution)/shard_map/phqk,kphd->qphd/dot_general | solution.py:65
  182.9 3.0 %copy.36 = bf16[8,64,10,64]{1,0,3,2:T(8,128)(2,1)} copy(bf16[8,64,10,64]{3,0,2,1:T(8,128)(2,1)} %fusion.5) | data formatting | bytes 1310720 | tf_op jit(solution)/shard_map/convert_element_type | solution.py:67
  186.0 2.1 reshape_reshape.7
  188.9 34.8 %all_to_all.9 = f32[8,64,640]{2,1,0:T(8,128)S(1)} all-to-all(f32[8,64,640]{2,1,0:T(8,128)S(1)} %bitcast.70), channel_id=1, replica_groups=mesh['groups'=2,'frame'=8,'row'=2] {'frame'}, dimensions={0} | all-to-all | bytes 2621440 | tf_op jit(solution)/shard_map/all_to_all | solution.py:129
  (52 shorter events, 11.4 us)
Async XLA Ops:
  6.5 64.1 %copy-start = (bf16[640,1920]{1,0:T(8,128)(2,1)S(1)}, bf16[640,1920]{1,0:T(8,128)(2,1)}, u32[]{:S(2)}) copy-start(bf16[640,1920]{1,0:T(8,128)(2,1)} %param.13) | copy-start | bytes 7372804
  6.5 78.8 %all-gather.3.cloned.1.call-start = ((), (), s32[]{:S(2)}) async-start(), calls=%async_computation.2 | async-start | bytes 1966080 | tf_op jit(solution)/shard_map/all_gather | solution.py:104
  45.2 14.6 %collective-permute-start.1 = (bf16[1,8,64,640]{3,2,1,0:T(8,128)(2,1)S(1)}, bf16[1,8,64,640]{3,2,1,0:T(8,128)(2,1)S(1)}, u32[]{:S(2)}, u32[]{:S(2)}) collective-permute-start(bf16[1,8,64,640]{3,2,1,0:T(8,128)(2,1)S(1)} %multiply_convert_fusion.1), channel_id=1, source_target_pairs={{2,0},{4,2},{6,4},{8,6},{10,8},{12,10},{14,12},{3,1},{5,3},{7,5},{... | collective-permute-start | bytes 1966088 | tf_op jit(solution)/shard_map/ppermute | solution.py:19
  46.5 22.9 %collective-permute-start = (bf16[1,8,64,640]{3,2,1,0:T(8,128)(2,1)S(1)}, bf16[1,8,64,640]{3,2,1,0:T(8,128)(2,1)S(1)}, u32[]{:S(2)}, u32[]{:S(2)}) collective-permute-start(bf16[1,8,64,640]{3,2,1,0:T(8,128)(2,1)S(1)} %multiply_convert_fusion.1), channel_id=1, source_target_pairs={{0,2},{2,4},{4,6},{6,8},{8,10},{10,12},{12,14},{1,3},{3,5},{5,7},{... | collective-permute-start | bytes 1966088 | tf_op jit(solution)/shard_map/ppermute | solution.py:16
  51.1 8.8 %copy-start.6 = (bf16[3,640,640]{2,1,0:T(8,128)(2,1)S(1)}, bf16[3,640,640]{2,1,0:T(8,128)(2,1)}, u32[]{:S(2)}) copy-start(bf16[3,640,640]{2,1,0:T(8,128)(2,1)} %param.11) | copy-start | bytes 7372804
  59.9 9.5 %copy-start.5 = (bf16[1,8,64,640]{3,2,1,0:T(8,128)(2,1)S(1)}, bf16[1,8,64,640]{3,2,1,0:T(8,128)(2,1)}, u32[]{:S(2)}) copy-start(bf16[1,8,64,640]{3,2,1,0:T(8,128)(2,1)} %param.9) | copy-start | bytes 1966084
  70.3 2.6 %copy-start.3 = (f32[512,640]{1,0:T(8,128)}, f32[512,640]{1,0:T(8,128)S(1)}, u32[]{:S(2)}) copy-start(f32[512,640]{1,0:T(8,128)S(1)} %get-tuple-element.20) | copy-start | bytes 3932164
  70.3 0.7 copy-start.10
  74.2 23.5 %all-gather.5.cloned.1.call-start = ((), (), s32[]{:S(2)}) async-start(), calls=%async_computation.3 | async-start | bytes 1966080 | tf_op jit(solution)/shard_map/all_gather | solution.py:105
  90.0 7.6 %copy-start.2 = (f32[10,512,1024]{2,1,0:T(8,128)}, f32[10,512,1024]{2,1,0:T(8,128)S(1)}, u32[]{:S(2)}) copy-start(f32[10,512,1024]{2,1,0:T(8,128)S(1)} %get-tuple-element.22) | copy-start | bytes 62914564
  100.2 9.5 %copy-start.4 = (f32[512,640]{1,0:T(8,128)S(1)}, f32[512,640]{1,0:T(8,128)}, u32[]{:S(2)}) copy-start(f32[512,640]{1,0:T(8,128)} %copy-done.3) | copy-start | bytes 3932164
  100.2 9.6 %copy-start.8 = (bf16[640,640]{1,0:T(8,128)(2,1)S(1)}, bf16[640,640]{1,0:T(8,128)(2,1)}, u32[]{:S(2)}) copy-start(bf16[640,640]{1,0:T(8,128)(2,1)} %param.14) | copy-start | bytes 2457604
  149.3 9.3 %copy-start.11 = (f32[640]{0:T(1024)S(1)}, f32[640]{0:T(1024)}, u32[]{:S(2)}) copy-start(f32[640]{0:T(1024)} %param.15) | copy-start | bytes 7684
  179.1 1.3 copy-start.7
  186.0 2.1 copy-start.9
  223.8 2.2 copy-start.1
Sparse Core Ops, SparseCore 0:
  74.3 11.0 all-gather.2
  86.9 10.5 all-gather.4
where the time goes:
time: 233 us
  blocking collectives  107 us (46%)
  local copies, waits for them, and re-layouts  32.5 us (14%)
  matrix products  28.6 us (12%)
  waiting for transfers between devices  26.2 us (11%)
  other arithmetic  18.6 us (8%)
  between operations  13.7 us (6%)
  starting transfers between devices  6.1 us (3%)
    all_to_all x1, blocking collectives, body(): lax.all_to_all(spaced, 'frame', split_axis=1, concat_axis=0, tiled=True)  37.4 us
    psum x1, blocking collectives, body(): first, second = lax.psum((first, second), ('frame', 'row'))  34.9 us
    all_to_all x1, blocking collectives, body(): lax.all_to_all(finished, 'frame', split_axis=0, concat_axis=1, tiled=True)  34.8 us
    unnamed x28, local copies, waits for them, and re-layouts  10.8 us
    all_gather x1, waiting for transfers between devices, body(): key_piece = lax.all_gather(key_rows, 'row', axis=1, tiled=True)  10.5 us
    dot_general x1, matrix products, body(): jnp.einsum('fhqk,fkhd->fhqd', weights, value_heads, preferred_element_typ...  9.53 us
    ppermute x1, waiting for transfers between devices, padded_2(): lax.ppermute(lax.slice_in_dim(block, block.shape[dim] - width, None, axis...  8.76 us
    reduce_sum x2, other arithmetic, layer_norm(): spread = jnp.mean(shifted * shifted, axis=-1, keepdims=True)  7.93 us
  transfers between devices with their start and end apart: 4, of which 3 were waited for; matrix products, arithmetic and copies ran while one was open for 5% of the time, Pallas kernels for 0%

commit v1 on v0

--- a/solution.py
+++ b/solution.py
@@ -85,7 +85,7 @@
     grouped = latent.astype(jnp.float32).reshape(frames, row_count, col_count, GROUPS, per_group)
     first = jnp.sum(grouped, axis=(0, 1, 2, 4))
     second = jnp.sum(grouped * grouped, axis=(0, 1, 2, 4))
-    first, second = lax.psum((first, second), ("frame", "row"))
+    first, second = lax.psum(lax.psum((first, second), "row"), "frame")
     number = frames * lax.axis_size("frame") * pixels * lax.axis_size("row") * per_group
     hidden = normalize_silu(grouped, first, second, number, norm_gain, latent.shape)
     padded = padded_2(hidden, (("frame", 0),), 1)

time: 233 us -> 224 us (0.961)
  blocking collectives: 107 us -> 97.8 us
    psum x1 -> x2, blocking collectives: 34.9 us -> 25.6 us  [body(): first, second = lax.psum(lax.psum((first, second), 'row'), 'frame')]
  transfers between devices with their start and end apart: 4 -> 4, of which waited for: 3 -> 3; matrix products, arithmetic and copies ran while one was open for 5% -> 6% of each run, Pallas kernels for 0% -> 0%
where the time goes in v1:
time: 224 us; the launch traced here: 223 us
  blocking collectives  97.8 us (44%)
  local copies, waits for them, and re-layouts  32.5 us (15%)
  matrix products  28.6 us (13%)
  waiting for transfers between devices  26.1 us (12%)
  other arithmetic  18.6 us (8%)
  between operations  13.7 us (6%)
  starting transfers between devices  6.1 us (3%)
    all_to_all x1, blocking collectives, body(): lax.all_to_all(spaced, 'frame', split_axis=1, concat_axis=0, tiled=True)  37.4 us
    all_to_all x1, blocking collectives, body(): lax.all_to_all(finished, 'frame', split_axis=0, concat_axis=1, tiled=True)  34.8 us
    psum x2, blocking collectives, body(): first, second = lax.psum(lax.psum((first, second), 'row'), 'frame')  25.6 us
    unnamed x28, local copies, waits for them, and re-layouts  10.8 us
    dot_general x1, matrix products, body(): jnp.einsum('fhqk,fkhd->fhqd', weights, value_heads, preferred_element_typ...  9.53 us
    ppermute x1, waiting for transfers between devices, padded_2(): lax.ppermute(lax.slice_in_dim(block, block.shape[dim] - width, None, axis...  9.53 us
    all_gather x1, waiting for transfers between devices, body(): key_piece = lax.all_gather(key_rows, 'row', axis=1, tiled=True)  9.31 us
    reduce_sum x2, other arithmetic, layer_norm(): spread = jnp.mean(shifted * shifted, axis=-1, keepdims=True)  7.93 us
  transfers between devices with their start and end apart: 4, of which 3 were waited for; matrix products, arithmetic and copies ran while one was open for 6% of the time, Pallas kernels for 0%

profile of v1, /device:TPU:0, one launch (start us, length us, event | category | flops | bytes accessed | tf_op | source)
XLA Modules:
  0.0 223.3 jit_solution(5120928171642902669)
XLA Ops:
  6.5 1.4 convert_reduce_fusion
  8.4 2.6 %all-reduce.1 = (f32[32]{0:T(128)S(1)}, f32[32]{0:T(128)S(1)}) all-reduce(f32[32]{0:T(128)S(1)} %reduce_sum.91, f32[32]{0:T(128)S(1)} %reduce_sum.88), channel_id=1, replica_groups=mesh['groups'=2,'frame'=8,'row'=2] {'row'}, use_global_device_ids=true, to_apply=%region_6.7 | all-reduce | flops 64 | bytes 512 | tf_op jit(solution)/shard_map/psum | solution.py:88
  11.0 22.9 %all-reduce = (f32[32]{0:T(128)S(1)}, f32[32]{0:T(128)S(1)}) all-reduce(f32[32]{0:T(128)S(1)} %get-tuple-element.9, f32[32]{0:T(128)S(1)} %get-tuple-element.10), channel_id=1, replica_groups=mesh['groups'=2,'frame'=8,'row'=2] {'frame'}, use_global_device_ids=true, to_apply=%region_7.8 | all-reduce | flops 64 | bytes 512 | tf_op jit(solution)/shard_map/psum | solution.py:88
  34.4 1.5 multiply_convert_fusion.1
  37.2 4.6 %collective-permute-start = (bf16[1,8,64,640]{3,2,1,0:T(8,128)(2,1)S(1)}, bf16[1,8,64,640]{3,2,1,0:T(8,128)(2,1)S(1)}, u32[]{:S(2)}, u32[]{:S(2)}) collective-permute-start(bf16[1,8,64,640]{3,2,1,0:T(8,128)(2,1)S(1)} %multiply_convert_fusion.1), channel_id=1, source_target_pairs={{0,2},{2,4},{4,6},{6,8},{8,10},{10,12},{12,14},{1,3},{3,5},{5,7},{... | collective-permute-start | bytes 1966088 | tf_op jit(solution)/shard_map/ppermute | solution.py:16
  41.8 2.0 fusion.24
  43.8 7.0 %collective-permute-done.1 = bf16[1,8,64,640]{3,2,1,0:T(8,128)(2,1)S(1)} collective-permute-done((bf16[1,8,64,640]{3,2,1,0:T(8,128)(2,1)S(1)}, bf16[1,8,64,640]{3,2,1,0:T(8,128)(2,1)S(1)}, u32[]{:S(2)}, u32[]{:S(2)}) %collective-permute-start.1) | collective-permute-done | bytes 655392 | tf_op jit(solution)/shard_map/ppermute | solution.py:19
  51.6 9.5 %collective-permute-done = bf16[1,8,64,640]{3,2,1,0:T(8,128)(2,1)S(1)} collective-permute-done((bf16[1,8,64,640]{3,2,1,0:T(8,128)(2,1)S(1)}, bf16[1,8,64,640]{3,2,1,0:T(8,128)(2,1)S(1)}, u32[]{:S(2)}, u32[]{:S(2)}) %collective-permute-start) | collective-permute-done | bytes 655392 | tf_op jit(solution)/shard_map/ppermute | solution.py:16
  62.7 1.9 fusion.4
  66.6 9.3 %all-gather.3.cloned.1.call-done = bf16[1,1024,640]{2,1,0:T(8,128)(2,1)} async-done(((bf16[1,512,640]{2,1,0:T(8,128)(2,1)}), bf16[1,1024,640]{2,1,0:T(8,128)(2,1)}) %all-gather.3.cloned.1.call-update) | async-done | bytes 1310736 | tf_op jit(solution)/shard_map/all_gather | solution.py:104
  75.9 1.6 copy.26
  77.5 3.0 %multiply_reduce_fusion = (f32[10,512]{1,0:T(8,128)S(1)}, f32[10,512,1024]{2,1,0:T(8,128)S(1)}) fusion(bf16[512,10,64]{0,2,1:T(8,128)(2,1)S(1)} %bitcast.75, bf16[1024,10,64]{0,2,1:T(8,128)(2,1)S(1)} %bitcast.69), kind=kOutput, calls=%fused_computation.1 | convolution fusion | flops 681569280 | bytes 22958080 | tf_op jit(solution)/shard_map/fqhd,fkhd->fhqk/dot_general | solution.py:109
  80.6 4.6 %fusion = f32[10,512]{1,0:T(8,128)S(1)} fusion(f32[10,512,1024]{2,1,0:T(8,128)S(1)} %get-tuple-element.24, f32[10,512]{1,0:T(8,128)S(1)} %get-tuple-element.23), kind=kLoop, calls=%fused_computation.2 | loop fusion | flops 15723520 | bytes 21012480 | tf_op jit(solution)/shard_map/reduce_sum | solution.py:115
  85.2 3.0 %copy-done.2 = f32[10,512,1024]{2,1,0:T(8,128)} copy-done((f32[10,512,1024]{2,1,0:T(8,128)}, f32[10,512,1024]{2,1,0:T(8,128)S(1)}, u32[]{:S(2)}) %copy-start.2) | copy-done | bytes 20971544
  88.2 2.5 %copy.27 = bf16[1,1024,640]{1,2,0:T(8,128)(2,1)} copy(bf16[1,1024,640]{2,1,0:T(8,128)(2,1)} %all-gather.5.cloned.1.call-done) | data formatting | bytes 2621440 | tf_op jit(solution)/shard_map/all_gather | solution.py:105
  90.7 9.5 %divide_convert_fusion = bf16[10,512,64]{1,2,0:T(8,128)(2,1)S(1)} fusion(bf16[1024,10,64]{0,2,1:T(8,128)(2,1)} %bitcast.78, f32[10,512,1024]{2,1,0:T(8,128)} %copy-done.2, f32[10,512]{1,0:T(8,128)S(1)} %get-tuple-element.23, f32[10,512]{1,0:T(8,128)S(1)} %get-tuple-element.18, f32[10,512]{1,0:T(8,128)S(1)} %get-tuple-element.17), kind=kOutput, calls=%fused_computation.28 | convolution fusion | flops 687800320 | bytes 22999040 | tf_op jit(solution)/shard_map/fhqk,fkhd->fhqd/dot_general | solution.py:117
  101.1 1.3 copy.28
  102.4 37.4 %all_to_all.8 = f32[1,512,640]{2,0,1:T(1,128)S(1)} all-to-all(f32[1,512,640]{2,0,1:T(1,128)S(1)} %copy.28), channel_id=1, replica_groups=mesh['groups'=2,'frame'=8,'row'=2] {'frame'}, dimensions={1} | all-to-all | bytes 2621440 | tf_op jit(solution)/shard_map/all_to_all | solution.py:124
  139.8 1.6 reduce_sum.95
  141.5 7.6 %multiply_reduce_fusion.2 = f32[512]{0:T(512)S(1)} fusion(f32[1,512,640]{2,0,1:T(1,128)S(1)} %all_to_all.8, f32[512]{0:T(512)S(1)} %broadcast_multiply_fusion), kind=kLoop, calls=%fused_computation.27 | loop fusion | flops 982528 | bytes 1314816 | tf_op jit(solution)/shard_map/reduce_sum | solution.py:35
  149.1 3.6 %convolution_convert_fusion = bf16[512,1920]{1,0:T(8,128)(2,1)S(1)} fusion(bf16[640,1920]{1,0:T(8,128)(2,1)} %param.16, f32[1,512,640]{2,0,1:T(1,128)S(1)} %all_to_all.8, f32[640]{0:T(1024)S(1)} %copy-done.11, f32[512]{0:T(512)S(1)} %add_rsqrt_fusion, f32[512]{0:T(512)S(1)} %broadcast_multiply_fusion), kind=kOutput, calls=%fused_computation.5 | convolution fusion | flops 1260584960 | bytes 5741056 | tf_op jit(solution)/shard_map/dot_general | solution.py:42
  153.8 2.3 %copy.40 = bf16[8,64,640]{1,2,0:T(8,128)(2,1)} copy(bf16[8,64,640]{2,1,0:T(8,128)(2,1)} %get-tuple-element.12) | data formatting | bytes 1310720
  156.1 2.6 %copy.32 = bf16[8,64,10,64]{3,0,2,1:T(8,128)(2,1)} copy(bf16[8,64,10,64]{1,3,2,0:T(8,128)(2,1)} %bitcast.71) | data formatting | bytes 1310720 | tf_op jit(solution)/shard_map/reshape | solution.py:56
  158.7 1.4 copy.41
  160.2 2.6 %copy.33 = bf16[8,64,10,64]{3,0,2,1:T(8,128)(2,1)} copy(bf16[8,64,10,64]{1,3,2,0:T(8,128)(2,1)} %bitcast.72) | data formatting | bytes 1310720 | tf_op jit(solution)/shard_map/reshape | solution.py:57
  162.8 1.4 copy.39
  164.2 2.7 %copy.34 = bf16[8,64,10,64]{3,0,2,1:T(8,128)(2,1)} copy(bf16[8,64,10,64]{1,3,2,0:T(8,128)(2,1)} %bitcast.73) | data formatting | bytes 1310720 | tf_op jit(solution)/shard_map/reshape | solution.py:58
  166.8 2.9 %multiply_reduce_fusion.1 = (f32[64,10,8]{2,1,0:T(8,128)S(1)}, f32[64,10,8,8]{2,3,1,0:T(8,128)S(1)}) fusion(bf16[8,64,10,64]{3,0,2,1:T(8,128)(2,1)} %copy.32, bf16[8,64,10,64]{3,0,2,1:T(8,128)(2,1)} %copy.33), kind=kOutput, calls=%fused_computation.11 | convolution fusion | flops 5319680 | bytes 1495040 | tf_op jit(solution)/shard_map/qphd,kphd->phqk/dot_general | solution.py:59
  171.0 2.5 %fusion.5 = bf16[8,64,10,64]{3,0,2,1:T(8,128)(2,1)} fusion(bf16[8,64,10,64]{3,0,2,1:T(8,128)(2,1)S(1)} %copy-done.7, f32[64,10,8,8]{2,3,1,0:T(8,128)S(1)} %get-tuple-element.26, f32[8,64,10]{0,2,1:T(8,128)S(1)} %bitcast.82, f32[64,10,8]{2,1,0:T(8,128)S(1)} %get-tuple-element.25), kind=kOutput, calls=%fused_computation.9 | convolution fusion | flops 6021120 | bytes 1515520 | tf_op jit(solution)/shard_map/phqk,kphd->qphd/dot_general | solution.py:65
  173.5 3.0 %copy.36 = bf16[8,64,10,64]{1,0,3,2:T(8,128)(2,1)} copy(bf16[8,64,10,64]{3,0,2,1:T(8,128)(2,1)} %fusion.5) | data formatting | bytes 1310720 | tf_op jit(solution)/shard_map/convert_element_type | solution.py:67
  176.5 2.1 reshape_reshape.7
  179.5 34.8 %all_to_all.9 = f32[8,64,640]{2,1,0:T(8,128)S(1)} all-to-all(f32[8,64,640]{2,1,0:T(8,128)S(1)} %bitcast.70), channel_id=1, replica_groups=mesh['groups'=2,'frame'=8,'row'=2] {'frame'}, dimensions={0} | all-to-all | bytes 2621440 | tf_op jit(solution)/shard_map/all_to_all | solution.py:129
  (53 shorter events, 12.7 us)
Async XLA Ops:
  6.5 55.8 %copy-start = (bf16[640,1920]{1,0:T(8,128)(2,1)S(1)}, bf16[640,1920]{1,0:T(8,128)(2,1)}, u32[]{:S(2)}) copy-start(bf16[640,1920]{1,0:T(8,128)(2,1)} %param.13) | copy-start | bytes 7372804
  6.5 69.4 %all-gather.3.cloned.1.call-start = ((), (), s32[]{:S(2)}) async-start(), calls=%async_computation.2 | async-start | bytes 1966080 | tf_op jit(solution)/shard_map/all_gather | solution.py:104
  35.9 14.9 %collective-permute-start.1 = (bf16[1,8,64,640]{3,2,1,0:T(8,128)(2,1)S(1)}, bf16[1,8,64,640]{3,2,1,0:T(8,128)(2,1)S(1)}, u32[]{:S(2)}, u32[]{:S(2)}) collective-permute-start(bf16[1,8,64,640]{3,2,1,0:T(8,128)(2,1)S(1)} %multiply_convert_fusion.1), channel_id=1, source_target_pairs={{2,0},{4,2},{6,4},{8,6},{10,8},{12,10},{14,12},{3,1},{5,3},{7,5},{... | collective-permute-start | bytes 1966088 | tf_op jit(solution)/shard_map/ppermute | solution.py:19
  37.2 23.9 %collective-permute-start = (bf16[1,8,64,640]{3,2,1,0:T(8,128)(2,1)S(1)}, bf16[1,8,64,640]{3,2,1,0:T(8,128)(2,1)S(1)}, u32[]{:S(2)}, u32[]{:S(2)}) collective-permute-start(bf16[1,8,64,640]{3,2,1,0:T(8,128)(2,1)S(1)} %multiply_convert_fusion.1), channel_id=1, source_target_pairs={{0,2},{2,4},{4,6},{6,8},{8,10},{10,12},{12,14},{1,3},{3,5},{5,7},{... | collective-permute-start | bytes 1966088 | tf_op jit(solution)/shard_map/ppermute | solution.py:16
  41.8 9.0 %copy-start.6 = (bf16[3,640,640]{2,1,0:T(8,128)(2,1)S(1)}, bf16[3,640,640]{2,1,0:T(8,128)(2,1)}, u32[]{:S(2)}) copy-start(bf16[3,640,640]{2,1,0:T(8,128)(2,1)} %param.11) | copy-start | bytes 7372804
  50.8 10.3 %copy-start.5 = (bf16[1,8,64,640]{3,2,1,0:T(8,128)(2,1)S(1)}, bf16[1,8,64,640]{3,2,1,0:T(8,128)(2,1)}, u32[]{:S(2)}) copy-start(bf16[1,8,64,640]{3,2,1,0:T(8,128)(2,1)} %param.9) | copy-start | bytes 1966084
  62.0 2.6 %copy-start.3 = (f32[512,640]{1,0:T(8,128)}, f32[512,640]{1,0:T(8,128)S(1)}, u32[]{:S(2)}) copy-start(f32[512,640]{1,0:T(8,128)S(1)} %get-tuple-element.22) | copy-start | bytes 3932164
  62.0 0.7 copy-start.10
  65.9 22.3 %all-gather.5.cloned.1.call-start = ((), (), s32[]{:S(2)}) async-start(), calls=%async_computation.3 | async-start | bytes 1966080 | tf_op jit(solution)/shard_map/all_gather | solution.py:105
  80.6 7.6 %copy-start.2 = (f32[10,512,1024]{2,1,0:T(8,128)}, f32[10,512,1024]{2,1,0:T(8,128)S(1)}, u32[]{:S(2)}) copy-start(f32[10,512,1024]{2,1,0:T(8,128)S(1)} %get-tuple-element.24) | copy-start | bytes 62914564
  90.7 9.5 %copy-start.4 = (f32[512,640]{1,0:T(8,128)S(1)}, f32[512,640]{1,0:T(8,128)}, u32[]{:S(2)}) copy-start(f32[512,640]{1,0:T(8,128)} %copy-done.3) | copy-start | bytes 3932164
  90.7 9.6 %copy-start.8 = (bf16[640,640]{1,0:T(8,128)(2,1)S(1)}, bf16[640,640]{1,0:T(8,128)(2,1)}, u32[]{:S(2)}) copy-start(bf16[640,640]{1,0:T(8,128)(2,1)} %param.14) | copy-start | bytes 2457604
  139.8 9.3 %copy-start.11 = (f32[640]{0:T(1024)S(1)}, f32[640]{0:T(1024)}, u32[]{:S(2)}) copy-start(f32[640]{0:T(1024)} %param.15) | copy-start | bytes 7684
  169.7 1.3 copy-start.7
  176.5 2.1 copy-start.9
  214.3 2.2 copy-start.1
Sparse Core Ops, SparseCore 0:
  66.0 9.8 all-gather.2
  77.5 10.5 all-gather.4
